TPU v7x, 32 devices: a whole 2x2x4 slice. The times are simulated.
32 devices in a mesh: dp: 4 (over z), mp: 8 (over y, x, core).
Axes of the slice: x: 2, y: 2, z: 4, core: 2. Of those that a mesh axis runs over, the one named last changes fastest.
Arguments:
- tokens: bfloat16 [8192, 2048], P(('dp', 'mp')), may hold values from -6 to 6
- segment: int32 [8192], P('dp'), may hold values from 0 to 2, as said below
- valid: int32 [8192], replicated, may hold values from 0 to 1
- gain_attn: float32 [2048], replicated, may hold values from 0.5 to 1.5
- w_query: bfloat16 [2048, 2048], P(None, 'mp'), may hold values from -0.125 to 0.125
- w_key: bfloat16 [2048, 2048], P(None, 'mp'), may hold values from -0.125 to 0.125
- w_value: bfloat16 [2048, 2048], P(None, 'mp'), may hold values from -0.125 to 0.125
- w_out: bfloat16 [2048, 2048], P('mp'), may hold values from -3 to 3
- gain_mlp: float32 [2048], replicated, may hold values from 0.5 to 1.5
- w_up: bfloat16 [2048, 8192], P(None, 'mp'), may hold values from -0.125 to 0.125
- w_down: bfloat16 [8192, 2048], P('mp'), may hold values from -0.0625 to 0.0625
- grad_out: bfloat16 [8192, 2048], P(('dp', 'mp')), may hold values from -6 to 6
Outputs:
- out_tokens: bfloat16 [8192, 2048], P(('dp', 'mp'))
- grad_tokens: bfloat16 [8192, 2048], P(('dp', 'mp'))
- grad_gain_attn: float32 [2048], P(('dp', 'mp'))
- grad_query: float32 [2048, 2048], P('dp', 'mp')
- grad_key: float32 [2048, 2048], P('dp', 'mp')
- grad_value: float32 [2048, 2048], P('dp', 'mp')
- grad_out_proj: float32 [2048, 2048], P('mp', 'dp')
- grad_gain_mlp: float32 [2048], P(('dp', 'mp'))
- grad_up: float32 [2048, 8192], P('dp', 'mp')
- grad_down: float32 [8192, 2048], P('mp', 'dp')
- rms_stream: float32 [], replicated
- rms_attn: float32 [], replicated
- rms_mlp: float32 [], replicated
Inputs may be any that keep to these rules, and one draw needn't show every extreme that they name: `segment`: within each slot the clip numbers never fall; clip 1 starts before position 128 of the slot and clip 2 starts at or after position 1921.
All inputs are finite; a program needn't handle non-finite values.
Results may differ from a plain program's by a relative error of at most 0.022.
Values may be sent and summed in bfloat16 or wider, within the bound.
A program may use at most 512 MiB of HBM per device.

v0:
```python
import jax
import jax.numpy as jnp
from jax import lax
from jax.sharding import PartitionSpec as P

D = 2048
HD = 128
EPSILON = 1e-05
NEGATIVE = -1e30


def norm_rows(values, norm_gain):
    scale = lax.rsqrt(jnp.mean(values * values, axis=-1, keepdims=True) + EPSILON)
    return values * scale * norm_gain


def norm_back(values, norm_gain, grad_norm):
    scale = lax.rsqrt(jnp.mean(values * values, axis=-1, keepdims=True) + EPSILON)
    normal = values * scale
    grad_hat = grad_norm * norm_gain
    inner = jnp.mean(grad_hat * normal, axis=-1, keepdims=True)
    return (scale * (grad_hat - normal * inner), normal)


def gelu_fn(values):
    return jax.nn.gelu(values, approximate=True)


def contract_rows(left_side, right_side):
    return lax.dot_general(
        left_side, right_side, (((0,), (0,)), ((), ())), preferred_element_type=jnp.float32
    )


def contract_cols(left_side, right_side):
    return lax.dot_general(
        left_side, right_side, (((1,), (1,)), ((), ())), preferred_element_type=jnp.float32
    )


def block_mask(first_row, row_count, segment_rows, valid_rows):
    rows_here = first_row + jnp.arange(row_count, dtype=jnp.int32)
    columns = jnp.arange(segment_rows.shape[0], dtype=jnp.int32)
    segment_here = lax.dynamic_slice_in_dim(segment_rows, first_row, row_count)
    same_clip = segment_here[:, None] == segment_rows[None, :]
    earlier = (columns[None, :] < rows_here[:, None]) & (valid_rows[None, :] > 0)
    itself = columns[None, :] == rows_here[:, None]
    return same_clip & (earlier | itself)


def attend_forward(queries, keys_all, values_all, segment_rows, valid_rows, head_count):
    seq_rows = queries.shape[0]
    block_rows = min(512, seq_rows)
    key_heads = keys_all.reshape(seq_rows, head_count, HD)
    value_heads = values_all.reshape(seq_rows, head_count, HD)

    def one_block(first_row):
        query_block = lax.dynamic_slice_in_dim(queries, first_row, block_rows, 0).reshape(
            block_rows, head_count, HD
        )
        scores = jnp.einsum(
            "qhd,khd->hqk", query_block, key_heads, preferred_element_type=jnp.float32
        ) * HD ** (-0.5)
        allowed = block_mask(first_row, block_rows, segment_rows, valid_rows)
        scores = jnp.where(allowed[None], scores, NEGATIVE)
        largest = jnp.max(scores, axis=-1, keepdims=True)
        powers = jnp.exp(scores - largest)
        row_total = jnp.sum(powers, axis=-1, keepdims=True)
        attention = (powers / row_total).astype(jnp.bfloat16)
        blended = jnp.einsum(
            "hqk,khd->qhd", attention, value_heads, preferred_element_type=jnp.float32
        )
        return (
            blended.astype(jnp.bfloat16).reshape(block_rows, head_count * HD),
            (largest + jnp.log(row_total))[:, :, 0],
        )

    starts = jnp.arange(seq_rows // block_rows, dtype=jnp.int32) * block_rows
    blended, logsum = lax.map(one_block, starts)
    return (blended.reshape(seq_rows, head_count * HD), logsum)


def attend_backward(
    queries, keys_all, values_all, logsum, grad_mixed, segment_rows, valid_rows, head_count
):
    seq_rows = queries.shape[0]
    block_rows = min(512, seq_rows)
    scale = HD ** (-0.5)
    key_heads = keys_all.reshape(seq_rows, head_count, HD)
    value_heads = values_all.reshape(seq_rows, head_count, HD)

    def one_block(running, block_item):
        grad_keys, grad_values = running
        first_row, block_logsum = block_item
        query_block = lax.dynamic_slice_in_dim(queries, first_row, block_rows, 0).reshape(
            block_rows, head_count, HD
        )
        grad_block = lax.dynamic_slice_in_dim(grad_mixed, first_row, block_rows, 0).reshape(
            block_rows, head_count, HD
        )
        scores = (
            jnp.einsum("qhd,khd->hqk", query_block, key_heads, preferred_element_type=jnp.float32)
            * scale
        )
        allowed = block_mask(first_row, block_rows, segment_rows, valid_rows)
        scores = jnp.where(allowed[None], scores, NEGATIVE)
        attention = jnp.exp(scores - block_logsum[:, :, None])
        grad_attention = jnp.einsum(
            "qhd,khd->hqk", grad_block, value_heads, preferred_element_type=jnp.float32
        )
        inner = jnp.sum(grad_attention * attention, axis=-1, keepdims=True)
        grad_scores = (attention * (grad_attention - inner)).astype(jnp.bfloat16)
        grad_query_block = (
            jnp.einsum("hqk,khd->qhd", grad_scores, key_heads, preferred_element_type=jnp.float32)
            * scale
        )
        grad_keys = (
            grad_keys
            + jnp.einsum(
                "hqk,qhd->khd", grad_scores, query_block, preferred_element_type=jnp.float32
            )
            * scale
        )
        grad_values = grad_values + jnp.einsum(
            "hqk,qhd->khd",
            attention.astype(jnp.bfloat16),
            grad_block,
            preferred_element_type=jnp.float32,
        )
        return ((grad_keys, grad_values), grad_query_block.reshape(block_rows, head_count * HD))

    starts = jnp.arange(seq_rows // block_rows, dtype=jnp.int32) * block_rows
    zeros_heads = jnp.zeros((seq_rows, head_count, HD), jnp.float32)
    (grad_keys, grad_values), grad_queries = lax.scan(
        one_block, (zeros_heads, zeros_heads), (starts, logsum)
    )
    width = head_count * HD
    return (
        grad_queries.reshape(seq_rows, width).astype(jnp.bfloat16),
        grad_keys.reshape(seq_rows, width).astype(jnp.bfloat16),
        grad_values.reshape(seq_rows, width).astype(jnp.bfloat16),
    )


def on_device(
    tokens,
    segment,
    valid,
    gain_attn,
    w_query,
    w_key,
    w_value,
    w_out,
    gain_mlp,
    w_up,
    w_down,
    grad_out,
):
    own_rows = tokens.shape[0]
    seq_rows = segment.shape[0]
    head_count = w_query.shape[1] // HD
    dp_index = lax.axis_index("dp")
    mp_index = lax.axis_index("mp")
    own_first = mp_index * own_rows
    valid_group = lax.dynamic_slice_in_dim(valid, dp_index * seq_rows, seq_rows)
    valid_own = lax.dynamic_slice_in_dim(valid_group, own_first, own_rows)
    token_values = tokens.astype(jnp.float32)
    gathered = lax.all_gather(tokens, "mp", axis=0, tiled=True)
    normed_attn = norm_rows(gathered.astype(jnp.float32), gain_attn).astype(jnp.bfloat16)
    queries = jnp.dot(normed_attn, w_query, preferred_element_type=jnp.float32).astype(jnp.bfloat16)
    keys_all = jnp.dot(normed_attn, w_key, preferred_element_type=jnp.float32).astype(jnp.bfloat16)
    values_all = jnp.dot(normed_attn, w_value, preferred_element_type=jnp.float32).astype(
        jnp.bfloat16
    )
    mixed, logsum = attend_forward(queries, keys_all, values_all, segment, valid_group, head_count)
    attn_rows = lax.psum(
        jnp.dot(mixed, w_out, preferred_element_type=jnp.float32).astype(jnp.bfloat16), "mp"
    ).astype(jnp.float32)
    residual_rows = gathered.astype(jnp.float32) + attn_rows
    attn_own = lax.dynamic_slice_in_dim(attn_rows, own_first, own_rows, 0)
    residual_own = lax.dynamic_slice_in_dim(residual_rows, own_first, own_rows, 0)
    normed_mlp = norm_rows(residual_rows, gain_mlp).astype(jnp.bfloat16)
    hidden_pre = jnp.dot(normed_mlp, w_up, preferred_element_type=jnp.float32)
    hidden = gelu_fn(hidden_pre).astype(jnp.bfloat16)
    mlp_own = lax.psum_scatter(
        jnp.dot(hidden, w_down, preferred_element_type=jnp.float32).astype(jnp.bfloat16),
        "mp",
        scatter_dimension=0,
        tiled=True,
    ).astype(jnp.float32)
    stream_own = residual_own + mlp_own
    out_tokens = stream_own.astype(jnp.bfloat16)
    mask_own = valid_own.astype(jnp.float32)[:, None]
    squares = lax.psum(
        (
            jnp.sum(mask_own * stream_own * stream_own),
            jnp.sum(mask_own * attn_own * attn_own),
            jnp.sum(mask_own * mlp_own * mlp_own),
        ),
        ("dp", "mp"),
    )
    counted = jnp.maximum(jnp.sum(valid).astype(jnp.float32) * D, 1.0)
    grad_rows = lax.all_gather(grad_out, "mp", axis=0, tiled=True)
    grad_hidden = contract_cols(grad_rows, w_down)
    grad_down = contract_rows(hidden, grad_rows)
    grad_pre = jax.vjp(gelu_fn, hidden_pre)[1](grad_hidden)[0].astype(jnp.bfloat16)
    grad_up = contract_rows(normed_mlp, grad_pre)
    grad_normed = lax.psum(contract_cols(grad_pre, w_up).astype(jnp.bfloat16), "mp").astype(
        jnp.float32
    )
    grad_input_rows, normal_rows = norm_back(residual_rows, gain_mlp, grad_normed)
    grad_resid_rows = grad_rows.astype(jnp.float32) + grad_input_rows
    grad_resid_own = lax.dynamic_slice_in_dim(grad_resid_rows, own_first, own_rows, 0)
    gain_mlp_part = jnp.sum(
        lax.dynamic_slice_in_dim(grad_normed * normal_rows, own_first, own_rows, 0), axis=0
    )
    grad_branch = grad_resid_rows.astype(jnp.bfloat16)
    grad_out_proj = contract_rows(mixed, grad_branch)
    grad_mixed = contract_cols(grad_branch, w_out).astype(jnp.bfloat16)
    grad_queries, grad_keys, grad_values = attend_backward(
        queries, keys_all, values_all, logsum, grad_mixed, segment, valid_group, head_count
    )
    grad_query = contract_rows(normed_attn, grad_queries)
    grad_key = contract_rows(normed_attn, grad_keys)
    grad_value = contract_rows(normed_attn, grad_values)
    total_term = contract_cols(grad_queries, w_query)
    total_term = total_term + contract_cols(grad_keys, w_key)
    grad_normed_attn = lax.psum_scatter(
        (total_term + contract_cols(grad_values, w_value)).astype(jnp.bfloat16),
        "mp",
        scatter_dimension=0,
        tiled=True,
    ).astype(jnp.float32)
    grad_input_attn, normal_attn = norm_back(token_values, gain_attn, grad_normed_attn)
    grad_tokens = (grad_resid_own + grad_input_attn).astype(jnp.bfloat16)
    gain_attn_part = jnp.sum(grad_normed_attn * normal_attn, axis=0)
    gain_grads = (
        lax.psum_scatter(gain_attn_part, ("dp", "mp"), scatter_dimension=0, tiled=True),
        lax.psum_scatter(gain_mlp_part, ("dp", "mp"), scatter_dimension=0, tiled=True),
    )
    inner_grads = (
        lax.psum_scatter(
            grad_query.astype(jnp.bfloat16), "dp", scatter_dimension=0, tiled=True
        ).astype(jnp.float32),
        lax.psum_scatter(
            grad_key.astype(jnp.bfloat16), "dp", scatter_dimension=0, tiled=True
        ).astype(jnp.float32),
        lax.psum_scatter(
            grad_value.astype(jnp.bfloat16), "dp", scatter_dimension=0, tiled=True
        ).astype(jnp.float32),
        lax.psum_scatter(
            grad_up.astype(jnp.bfloat16), "dp", scatter_dimension=0, tiled=True
        ).astype(jnp.float32),
    )
    outer_grads = (
        lax.psum_scatter(
            grad_out_proj.astype(jnp.bfloat16), "dp", scatter_dimension=1, tiled=True
        ).astype(jnp.float32),
        lax.psum_scatter(
            grad_down.astype(jnp.bfloat16), "dp", scatter_dimension=1, tiled=True
        ).astype(jnp.float32),
    )
    return (
        out_tokens,
        grad_tokens,
        gain_grads[0],
        inner_grads[0],
        inner_grads[1],
        inner_grads[2],
        outer_grads[0],
        gain_grads[1],
        inner_grads[3],
        outer_grads[1],
        jnp.sqrt(squares[0] / counted),
        jnp.sqrt(squares[1] / counted),
        jnp.sqrt(squares[2] / counted),
    )


def solution(mesh):
    placed = (
        P(("dp", "mp"), None),
        P("dp"),
        P(),
        P(),
        P(None, "mp"),
        P(None, "mp"),
        P(None, "mp"),
        P("mp", None),
        P(),
        P(None, "mp"),
        P("mp", None),
        P(("dp", "mp"), None),
    )
    return jax.shard_map(
        on_device,
        mesh=mesh,
        in_specs=placed,
        out_specs=(
            P(("dp", "mp"), None),
            P(("dp", "mp"), None),
            P(("dp", "mp")),
            P("dp", "mp"),
            P("dp", "mp"),
            P("dp", "mp"),
            P("mp", "dp"),
            P(("dp", "mp")),
            P("dp", "mp"),
            P("mp", "dp"),
            P(),
            P(),
            P(),
        ),
        check_vma=False,
    )
```

profile of v0, /device:TPU:0, one launch (start us, length us, event | category | flops | bytes accessed | tf_op | source)
XLA Modules:
  0.0 1085.7 jit_solution(5463557942506468040)
XLA Ops:
  8.8 58.3 %all-gather.3.cloned.1.call-done = bf16[2048,2048]{1,0:T(8,128)(2,1)} async-done(((bf16[256,2048]{1,0:T(8,128)(2,1)}), bf16[2048,2048]{1,0:T(8,128)(2,1)}) %all-gather.3.cloned.1.call-update) | async-done | bytes 8388624 | tf_op jit(solution)/shard_map/all_gather | solution.py:168
  72.2 8.7 fusion.28
  80.9 6.9 convolution_convert_fusion.8
  99.9 67.6 %while.27 = (s32[]{:T(128)}, bf16[4,512,256]{2,1,0:T(8,128)(2,1)}, f32[4,2,512]{2,1,0:T(2,128)S(1)}, s32[4]{0:T(128)S(1)}, s32[2048]{0:T(1024)S(1)}, /*index=5*/...) while((s32[]{:T(128)}, bf16[4,512,256]{2,1,0:T(8,128)(2,1)}, ...), condition=%wide.region_4.5_spmd, body=%wide.region_1.4_spmd.sunk | while | flops 1105331712 | bytes 37812440 | solution.py:79
  167.5 7.2 convolution_convert_fusion.2
  174.8 14.7 %fusion.62 = f32[2048,1024]{1,0:T(8,128)} fusion(bf16[2048,2048]{1,0:T(8,128)(2,1)} %all-gather.5.cloned.1.call-done, bf16[1024,2048]{1,0:T(8,128)(2,1)} %param.26), kind=kOutput, calls=%fused_computation.115 | convolution fusion | flops 8589934592 | bytes 20971520 | tf_op jit(solution)/shard_map/dot_general | solution.py:36
  189.5 112.2 %all-reduce.6.cloned.1.call-done = bf16[2048,2048]{1,0:T(8,128)(2,1)} async-done(((bf16[2048,2048]{1,0:T(8,128)(2,1)}), bf16[2048,2048]{1,0:T(8,128)(2,1)}) %all-reduce.6.cloned.1.call-update) | async-done | bytes 8388624 | tf_op jit(solution)/shard_map/psum | solution.py:176
  301.7 13.7 %convert_add_fusion = (f32[2048,2048]{1,0:T(8,128)}, f32[2048]{0:T(1024)S(1)}) fusion(bf16[2048,2048]{1,0:T(8,128)(2,1)} %all-gather.3.cloned.1.call-done, bf16[2048,2048]{1,0:T(8,128)(2,1)} %all-reduce.6.cloned.1.call-done), kind=kLoop, calls=%fused_computation.44 | loop fusion | flops 20969472 | bytes 33562624 | tf_op jit(solution)/shard_map/add | solution.py:179
  315.4 10.7 broadcast_multiply_fusion
  326.1 20.0 %fusion.35 = (bf16[2048,1024]{1,0:T(8,128)(2,1)S(1)}, f32[2048,1024]{1,0:T(8,128)}) fusion(f32[2048,1024]{1,0:T(8,128)} %fusion.62, bf16[2048,1024]{1,0:T(8,128)(2,1)S(1)} %copy-done.27, f32[2048,2048]{1,0:T(8,128)} %broadcast_multiply_fusion, f32[2048]{0:T(1024)S(1)} %copy-done.25), kind=kOutput, calls=%fused_computation.63 | convolution fusion | flops 8640266240 | bytes 41951232 | tf_op jit(solution)/shard_map/dot_general | solution.py:183
  348.0 11.3 %convolution_convert_fusion = bf16[2048,2048]{1,0:T(8,128)(2,1)} fusion(bf16[2048,1024]{1,0:T(8,128)(2,1)S(1)} %get-tuple-element.291, bf16[2048,1024]{1,0:T(8,128)(2,1)S(1)} %copy-done.27), kind=kOutput, calls=%fused_computation.66 | convolution fusion | flops 8594128896 | bytes 16777216 | tf_op jit(solution)/shard_map/dot_general | solution.py:36
  361.7 124.6 %all-reduce.8.cloned.1.call-done = bf16[2048,2048]{1,0:T(8,128)(2,1)} async-done(((bf16[2048,2048]{1,0:T(8,128)(2,1)}), bf16[2048,2048]{1,0:T(8,128)(2,1)}) %all-reduce.8.cloned.1.call-update) | async-done | bytes 8388624 | tf_op jit(solution)/shard_map/psum | solution.py:208
  486.3 9.2 multiply_reduce_fusion.1
  495.5 12.6 %multiply_add_fusion = f32[2048,2048]{1,0:T(8,128)S(1)} fusion(f32[2048,2048]{1,0:T(8,128)} %broadcast_multiply_fusion, bf16[2048,2048]{1,0:T(8,128)(2,1)} %all-gather.5.cloned.1.call-done, f32[2048]{0:T(1024)S(1)} %broadcast_multiply_fusion.1, bf16[2048,2048]{1,0:T(8,128)(2,1)} %all-reduce.8.cloned.1.call-done, f32[2048]{0:T(1024)S(1)} %copy-done.25, ...), kind=kLoop, calls=%fused_computation.51 | loop fusion | flops 29360128 | bytes 50356224 | tf_op jit(solution)/shard_map/add | solution.py:212
  517.1 9.1 fusion.43
  526.3 100.4 %while.28 = (s32[]{:T(128)}, f32[2048,2,128]{0,2,1:T(8,128)S(1)}, f32[2048,2,128]{0,2,1:T(8,128)}, bf16[4,512,256]{2,1,0:T(8,128)(2,1)}, s32[4]{0:T(128)S(1)}, /...) while((s32[]{:T(128)}, f32[2048,2,128]{0,2,1:T(8,128)S(1)}, ...), condition=%wide.region_13.14_spmd.clone, body=%wide.region_11.13_spmd.clone.sunk | while | flops 2724988416 | bytes 107800928 | solution.py:134
  626.8 7.1 convolution_convert_fusion.7
  634.1 6.9 convolution_convert_fusion.6
  642.8 6.9 convolution_convert_fusion.5
  649.8 15.4 %convolution_convert_fusion.4 = bf16[2048,1024]{1,0:T(8,128)(2,1)} fusion(bf16[2048,1024]{1,0:T(8,128)(2,1)} %copy-done.28, f32[2048,2048]{1,0:T(8,128)} %broadcast_multiply_fusion, f32[2048]{0:T(1024)S(1)} %copy-done.26), kind=kOutput, calls=%fused_computation.74 | convolution fusion | flops 8600420352 | bytes 25174016 | tf_op jit(solution)/shard_map/dot_general | solution.py:30
  665.3 16.3 %convolution_convert_fusion.3 = bf16[1024,2048]{1,0:T(8,128)(2,1)} fusion(bf16[2048,2048]{1,0:T(8,128)(2,1)} %all-gather.5.cloned.1.call-done, f32[2048,1024]{1,0:T(8,128)} %get-tuple-element.292), kind=kOutput, calls=%fused_computation.73 | convolution fusion | flops 8610906112 | bytes 20971520 | tf_op jit(solution)/shard_map/dot_general | solution.py:30
  681.6 15.7 %convolution_convert_fusion.1 = bf16[2048,2048]{1,0:T(8,128)(2,1)} fusion(bf16[1024,2048]{1,0:T(8,128)(2,1)} %param.26, f32[2048,1024]{1,0:T(8,128)} %get-tuple-element.292), kind=kOutput, calls=%fused_computation.67 | convolution fusion | flops 8613003264 | bytes 20971520 | tf_op jit(solution)/shard_map/dot_general | solution.py:186
  698.5 8.2 fusion.64
  706.8 8.1 fusion.63
  714.8 16.4 %add_convert_fusion = bf16[2048,2048]{1,0:T(8,128)(2,1)} fusion(f32[2048,2048]{1,0:T(8,128)} %fusion.63, f32[2048,2048]{1,0:T(8,128)} %fusion.64, bf16[2048,256]{0,1:T(8,128)(2,1)S(1)} %bitcast.131, bf16[2048,256]{1,0:T(8,128)(2,1)S(1)} %copy-done.19), kind=kOutput, calls=%fused_computation.50 | convolution fusion | flops 2160066560 | bytes 44040192 | tf_op jit(solution)/shard_map/dot_general | solution.py:36
  733.7 11.3 %convert_element_type.148 = f32[2048,2048]{1,0:T(8,128)} convert(bf16[2048,2048]{1,0:T(8,128)(2,1)} %all-reduce.6.cloned.1.call-done) | non-fusion elementwise | flops 4194304 | bytes 25165824 | tf_op jit(solution)/shard_map/convert_element_type | solution.py:178
  745.0 11.4 %convert_element_type.157 = f32[2048,2048]{1,0:T(8,128)} convert(bf16[2048,2048]{1,0:T(8,128)(2,1)} %all-reduce.8.cloned.1.call-done) | non-fusion elementwise | flops 4194304 | bytes 25165824 | tf_op jit(solution)/shard_map/convert_element_type | solution.py:208
  766.1 30.6 %reduce-scatter.21.cloned.1.call-done = bf16[512,1024]{1,0:T(8,128)(2,1)} async-done(((bf16[2048,1024]{1,0:T(8,128)(2,1)}), bf16[512,1024]{1,0:T(8,128)(2,1)}) %reduce-scatter.21.cloned.1.call-update) | async-done | bytes 1048592 | tf_op jit(solution)/shard_map/reduce_scatter | solution.py:251
  799.5 76.7 %reduce-scatter.23.cloned.1.call-done = bf16[1024,512]{1,0:T(8,128)(2,1)} async-done(((bf16[1024,2048]{1,0:T(8,128)(2,1)}), bf16[1024,512]{1,0:T(8,128)(2,1)}) %reduce-scatter.23.cloned.1.call-update) | async-done | bytes 1048592 | tf_op jit(solution)/shard_map/reduce_scatter | solution.py:259
  879.0 72.4 %reduce-scatter.9.cloned.1.call-done = bf16[256,2048]{1,0:T(8,128)(2,1)} async-done(((bf16[2048,2048]{1,0:T(8,128)(2,1)}), bf16[256,2048]{1,0:T(8,128)(2,1)}) %reduce-scatter.9.cloned.1.call-update) | async-done | bytes 1048592 | tf_op jit(solution)/shard_map/reduce_scatter | solution.py:185
  956.4 70.1 %reduce-scatter.11.cloned.1.call-done = bf16[256,2048]{1,0:T(8,128)(2,1)} async-done(((bf16[2048,2048]{1,0:T(8,128)(2,1)}), bf16[256,2048]{1,0:T(8,128)(2,1)}) %reduce-scatter.11.cloned.1.call-update) | async-done | bytes 1048592 | tf_op jit(solution)/shard_map/reduce_scatter | solution.py:228
  1028.5 39.9 %all-reduce.2 = (f32[2048]{0:T(1024)S(1)}, f32[2048]{0:T(1024)S(1)}, f32[]{:T(128)}, f32[]{:T(128)}, f32[]{:T(128)}) all-reduce(f32[2048]{0:T(1024)S(1)} %get-tuple-element.232, f32[2048]{0:T(1024)S(1)} %fusion.59, f32[]{:T(128)} %get-tuple-element.235, f32[]{:T(128)} %get-tuple-element.236, ...), channel_id=4, replica_groups=mesh['dp'=4,'mp'=8] {'dp','mp'}, use_global_device_ids=true, to_apply=%region_17.18.clone | all-reduce | flops 4099 | bytes 32792
  (270 shorter events, 215.5 us)
Async XLA Ops:
  7.2 160.3 %copy-start = (bf16[256,2048]{1,0:T(8,128)(2,1)S(1)}, bf16[256,2048]{1,0:T(8,128)(2,1)}, u32[]{:S(2)}) copy-start(bf16[256,2048]{1,0:T(8,128)(2,1)} %param.23) | copy-start | bytes 3145732
  7.2 65.0 %copy-start.23 = (f32[2048]{0:T(1024)S(1)}, f32[2048]{0:T(1024)}, u32[]{:S(2)}) copy-start(f32[2048]{0:T(1024)} %param.19) | copy-start | bytes 24580
  7.2 59.8 %all-gather.3.cloned.1.call-start = ((), (), s32[]{:S(2)}) async-start(), calls=%async_computation.8 | async-start | bytes 9437184 | tf_op jit(solution)/shard_map/all_gather | solution.py:168
  7.9 166.9 %all-gather.5.cloned.1.call-start = ((), (), s32[]{:S(2)}) async-start(), calls=%async_computation.11 | async-start | bytes 9437184 | tf_op jit(solution)/shard_map/all_gather | solution.py:203
  8.7 293.0 %all-reduce.6.cloned.1.call-start = ((), (), s32[]{:S(2)}) async-start(), calls=%async_computation.9 | async-start | bytes 16777216 | tf_op jit(solution)/shard_map/psum | solution.py:176
  72.2 8.7 copy-start.18
  90.2 8.2 copy-start.4
  91.7 8.2 copy-start.13
  91.7 8.2 dynamic-slice-start
  167.5 7.3 copy-start.8
  174.7 311.5 %all-reduce.8.cloned.1.call-start = ((), (), s32[]{:S(2)}) async-start(), calls=%async_computation.12 | async-start | bytes 16777216 | tf_op jit(solution)/shard_map/psum | solution.py:208
  301.7 13.7 %copy-start.3 = (bf16[2048,2048]{1,0:T(8,128)(2,1)S(1)}, bf16[2048,2048]{1,0:T(8,128)(2,1)}, u32[]{:S(2)}) copy-start(bf16[2048,2048]{1,0:T(8,128)(2,1)} %all-reduce.6.cloned.1.call-done) | copy-start | bytes 25165828
  315.4 10.7 copy-start.25
  315.4 10.7 copy-start.27
  359.4 399.5 %reduce-scatter.19.cloned.1.call-start = ((), (), s32[]{:S(2)}) async-start(), calls=%async_computation.17 | async-start | bytes 1310720 | tf_op jit(solution)/shard_map/reduce_scatter | solution.py:256
  495.5 18.3 %copy-start.10 = (bf16[4,512,256]{2,1,0:T(8,128)(2,1)S(1)}, bf16[4,512,256]{2,1,0:T(8,128)(2,1)}, u32[]{:S(2)}) copy-start(bf16[4,512,256]{2,1,0:T(8,128)(2,1)} %get-tuple-element.125) | copy-start | bytes 3145732
  526.3 234.4 %reduce-scatter.13.cloned.1.call-start = ((), (), s32[]{:S(2)}) async-start(), calls=%async_computation.14 | async-start | bytes 1310720 | tf_op jit(solution)/shard_map/reduce_scatter | solution.py:242
  531.0 7.5 copy-start.11
  556.0 7.5 copy-start.11
  581.0 7.5 copy-start.11
  606.0 7.5 copy-start.11
  633.9 128.6 %reduce-scatter.15.cloned.1.call-start = ((), (), s32[]{:S(2)}) async-start(), calls=%async_computation.15 | async-start | bytes 1310720 | tf_op jit(solution)/shard_map/reduce_scatter | solution.py:245
  641.0 123.3 %reduce-scatter.17.cloned.1.call-start = ((), (), s32[]{:S(2)}) async-start(), calls=%async_computation.16 | async-start | bytes 1310720 | tf_op jit(solution)/shard_map/reduce_scatter | solution.py:248
  649.7 146.9 %reduce-scatter.21.cloned.1.call-start = ((), (), s32[]{:S(2)}) async-start(), calls=%async_computation.18 | async-start | bytes 5242880 | tf_op jit(solution)/shard_map/reduce_scatter | solution.py:251
  665.2 210.9 %reduce-scatter.23.cloned.1.call-start = ((), (), s32[]{:S(2)}) async-start(), calls=%async_computation.19 | async-start | bytes 5242880 | tf_op jit(solution)/shard_map/reduce_scatter | solution.py:259
  681.6 269.8 %reduce-scatter.9.cloned.1.call-start = ((), (), s32[]{:S(2)}) async-start(), calls=%async_computation.10 | async-start | bytes 9437184 | tf_op jit(solution)/shard_map/reduce_scatter | solution.py:185
  697.3 329.1 %reduce-scatter.11.cloned.1.call-start = ((), (), s32[]{:S(2)}) async-start(), calls=%async_computation.13 | async-start | bytes 9437184 | tf_op jit(solution)/shard_map/reduce_scatter | solution.py:228
  698.5 8.2 copy-start.17
  698.5 8.2 copy-start.20
  706.8 8.1 copy-start.19
  758.9 267.6 %copy-start.24 = (f32[2048]{0:T(1024)S(1)}, f32[2048]{0:T(1024)}, u32[]{:S(2)}) copy-start(f32[2048]{0:T(1024)} %param.19) | copy-start | bytes 24580
  796.6 278.6 %copy-start.1 = (bf16[256,2048]{1,0:T(8,128)(2,1)S(1)}, bf16[256,2048]{1,0:T(8,128)(2,1)}, u32[]{:S(2)}) copy-start(bf16[256,2048]{1,0:T(8,128)(2,1)} %param.23) | copy-start | bytes 3145732
  (25 other events, 98.7 us)
Sparse Core Ops, SparseCore 0:
  9.9 57.0 all-gather.2
  68.9 54.3 all-gather.4
  174.9 126.7 all-reduce.5
  359.5 126.7 all-reduce.7
  526.4 27.3 reduce-scatter.18
  634.0 27.3 reduce-scatter.12
  664.2 25.7 reduce-scatter.14
  693.0 25.7 reduce-scatter.16
  721.2 75.4 reduce-scatter.20
  798.9 77.2 reduce-scatter.22
  879.6 71.7 reduce-scatter.8
  955.1 71.2 reduce-scatter.10
where the time goes:
time: 1090 us
  waiting for transfers between devices  546 us (50%)
  matrix products  256 us (23%)
  other arithmetic  167 us (15%)
  blocking collectives  39.9 us (4%)
  local copies, waits for them, and re-layouts  38.6 us (4%)
  between operations  20.9 us (2%)
  loops' own time  16.8 us (2%)
    psum x1, waiting for transfers between devices, on_device(): lax.psum(contract_cols(grad_pre, w_up).astype(jnp.bfloat16), 'mp')  125 us
    psum x1, waiting for transfers between devices, on_device(): lax.psum(jnp.dot(mixed, w_out, preferred_element_type=jnp.float32).astype...  112 us
    reduce_scatter x1, waiting for transfers between devices, on_device(): lax.psum_scatter(grad_down.astype(jnp.bfloat16), 'dp', scatter_dimension=...  76.7 us
    reduce_scatter x1, waiting for transfers between devices, on_device(): lax.psum_scatter(jnp.dot(hidden, w_down, preferred_element_type=jnp.float...  72.4 us
    reduce_scatter x1, waiting for transfers between devices, on_device(): lax.psum_scatter((total_term + contract_cols(grad_values, w_value)).astyp...  70.1 us
    dot_general x6, matrix products, contract_cols(): lax.dot_general(left_side, right_side, (((1,), (1,)), ((), ())), preferre...  67.8 us
    all_gather x1, waiting for transfers between devices, on_device(): gathered = lax.all_gather(tokens, 'mp', axis=0, tiled=True)  58.3 us
    dot_general x6, matrix products, contract_rows(): lax.dot_general(left_side, right_side, (((0,), (0,)), ((), ())), preferre...  55.9 us
  transfers between devices with their start and end apart: 12, of which 7 were waited for; matrix products, arithmetic and copies ran while one was open for 33% of the time, Pallas kernels for 0%

commit v1 on v0

--- a/solution.py
+++ b/solution.py
@@ -165,7 +165,24 @@
     valid_group = lax.dynamic_slice_in_dim(valid, dp_index * seq_rows, seq_rows)
     valid_own = lax.dynamic_slice_in_dim(valid_group, own_first, own_rows)
     token_values = tokens.astype(jnp.float32)
-    gathered = lax.all_gather(tokens, "mp", axis=0, tiled=True)
+    peers, position, rows = (lax.axis_size("mp"), lax.axis_index("mp"), tokens.shape[0])
+    ahead = [(i, (i + 1) % peers) for i in range(peers)]
+    left = [(i, (i - 1) % peers) for i in range(peers)]
+    out = jnp.zeros((*tokens.shape[:0], peers * rows, *tokens.shape[0 + 1 :]), tokens.dtype)
+    out = lax.dynamic_update_slice_in_dim(out, tokens, position * rows, axis=0)
+    from_left = from_right = tokens
+    middle = peers // 2
+    for lap in range(1, middle + 1):
+        from_left = lax.ppermute(from_left, "mp", ahead)
+        out = lax.dynamic_update_slice_in_dim(
+            out, from_left, (position - lap) % peers * rows, axis=0
+        )
+        if lap < peers - middle:
+            from_right = lax.ppermute(from_right, "mp", left)
+            out = lax.dynamic_update_slice_in_dim(
+                out, from_right, (position + lap) % peers * rows, axis=0
+            )
+    gathered = out
     normed_attn = norm_rows(gathered.astype(jnp.float32), gain_attn).astype(jnp.bfloat16)
     queries = jnp.dot(normed_attn, w_query, preferred_element_type=jnp.float32).astype(jnp.bfloat16)
     keys_all = jnp.dot(normed_attn, w_key, preferred_element_type=jnp.float32).astype(jnp.bfloat16)

time: 1090 us -> 1180 us (1.083)
  waiting for transfers between devices: 546 us -> 612 us
    ppermute x0 -> x7, waiting for transfers between devices: none -> 72.9 us  [the longest x4 71.2 us: on_device(): from_left = lax.ppermute(from_left, 'mp', ahead)]
    all_gather x1 -> x0, waiting for transfers between devices: 58.3 us -> none  [on_device(): gathered = lax.all_gather(tokens, 'mp', axis=0, tiled=True)]
    all_gather x1, waiting for transfers between devices: 0.02 us -> 31.5 us  [on_device(): grad_rows = lax.all_gather(grad_out, 'mp', axis=0, tiled=True)]
    psum x1, waiting for transfers between devices: 112 us -> 133 us  [on_device(): lax.psum(jnp.dot(mixed, w_out, preferred_element_type=jnp.float32).astype...]
  transfers between devices with their start and end apart: 12 -> 18, of which waited for: 7 -> 13; matrix products, arithmetic and copies ran while one was open for 33% -> 23% of each run, Pallas kernels for 0% -> 0%
where the time goes in v1:
time: 1180 us; the launch traced here: 1170 us
  waiting for transfers between devices  612 us (52%)
  matrix products  255 us (22%)
  other arithmetic  164 us (14%)
  local copies, waits for them, and re-layouts  47.6 us (4%)
  blocking collectives  39.9 us (3%)
  between operations  20.8 us (2%)
  loops' own time  17.1 us (1%)
    psum x1, waiting for transfers between devices, on_device(): lax.psum(jnp.dot(mixed, w_out, preferred_element_type=jnp.float32).astype...  133 us
    psum x1, waiting for transfers between devices, on_device(): lax.psum(contract_cols(grad_pre, w_up).astype(jnp.bfloat16), 'mp')  124 us
    reduce_scatter x1, waiting for transfers between devices, on_device(): lax.psum_scatter(grad_down.astype(jnp.bfloat16), 'dp', scatter_dimension=...  76.8 us
    reduce_scatter x1, waiting for transfers between devices, on_device(): lax.psum_scatter(jnp.dot(hidden, w_down, preferred_element_type=jnp.float...  72.3 us
    ppermute x4, waiting for transfers between devices, on_device(): from_left = lax.ppermute(from_left, 'mp', ahead)  71.2 us
    reduce_scatter x1, waiting for transfers between devices, on_device(): lax.psum_scatter((total_term + contract_cols(grad_values, w_value)).astyp...  70.2 us
    dot_general x6, matrix products, contract_cols(): lax.dot_general(left_side, right_side, (((1,), (1,)), ((), ())), preferre...  67.7 us
    dot_general x6, matrix products, contract_rows(): lax.dot_general(left_side, right_side, (((0,), (0,)), ((), ())), preferre...  55.8 us
  transfers between devices with their start and end apart: 18, of which 13 were waited for; matrix products, arithmetic and copies ran while one was open for 23% of the time, Pallas kernels for 0%

profile of v1, /device:TPU:0, one launch (start us, length us, event | category | flops | bytes accessed | tf_op | source)
XLA Modules:
  0.0 1167.3 jit_solution(8582457588591752917)
XLA Ops:
  10.7 21.2 %collective-permute-done = bf16[256,2048]{1,0:T(8,128)(2,1)S(1)} collective-permute-done((bf16[256,2048]{1,0:T(8,128)(2,1)}, bf16[256,2048]{1,0:T(8,128)(2,1)S(1)}, u32[]{:S(2)}, u32[]{:S(2)}) %collective-permute-start) | collective-permute-done | bytes 1048608 | tf_op jit(solution)/shard_map/ppermute | solution.py:176
  36.2 19.5 %collective-permute-done.2 = bf16[256,2048]{1,0:T(8,128)(2,1)} collective-permute-done((bf16[256,2048]{1,0:T(8,128)(2,1)S(1)}, bf16[256,2048]{1,0:T(8,128)(2,1)}, u32[]{:S(2)}, u32[]{:S(2)}) %collective-permute-start.2) | collective-permute-done | bytes 1048608 | tf_op jit(solution)/shard_map/ppermute | solution.py:176
  60.9 19.4 %collective-permute-done.4 = bf16[256,2048]{1,0:T(8,128)(2,1)} collective-permute-done((bf16[256,2048]{1,0:T(8,128)(2,1)}, bf16[256,2048]{1,0:T(8,128)(2,1)}, u32[]{:S(2)}, u32[]{:S(2)}) %collective-permute-start.4) | collective-permute-done | bytes 1048608 | tf_op jit(solution)/shard_map/ppermute | solution.py:176
  84.6 11.1 collective-permute-done.6
  100.7 8.7 fusion.28
  128.5 67.6 %while.27 = (s32[]{:T(128)}, bf16[4,512,256]{2,1,0:T(8,128)(2,1)}, f32[4,2,512]{2,1,0:T(2,128)S(1)}, s32[4]{0:T(128)S(1)}, s32[2048]{0:T(1024)S(1)}, /*index=5*/...) while((s32[]{:T(128)}, bf16[4,512,256]{2,1,0:T(8,128)(2,1)}, ...), condition=%wide.region_4.5_spmd, body=%wide.region_1.4_spmd.sunk | while | flops 1105331712 | bytes 37812440 | solution.py:79
  196.0 7.2 convolution_convert_fusion.2
  204.0 132.5 %all-reduce.6.cloned.1.call-done = bf16[2048,2048]{1,0:T(8,128)(2,1)} async-done(((bf16[2048,2048]{1,0:T(8,128)(2,1)}), bf16[2048,2048]{1,0:T(8,128)(2,1)}) %all-reduce.6.cloned.1.call-update) | async-done | bytes 8388624 | tf_op jit(solution)/shard_map/psum | solution.py:193
  336.6 14.7 %convert_add_fusion = (f32[2048,2048]{1,0:T(8,128)}, f32[2048]{0:T(1024)S(1)}) fusion(bf16[2048,2048]{1,0:T(8,128)(2,1)} %copy-done.3, bf16[2048,2048]{1,0:T(8,128)(2,1)} %all-reduce.6.cloned.1.call-done), kind=kLoop, calls=%fused_computation.44 | loop fusion | flops 20969472 | bytes 33562624 | tf_op jit(solution)/shard_map/add | solution.py:196
  351.3 10.4 broadcast_multiply_fusion
  361.7 31.5 %all-gather.2.cloned.1.call-done = bf16[2048,2048]{1,0:T(8,128)(2,1)} async-done(((bf16[256,2048]{1,0:T(8,128)(2,1)}), bf16[2048,2048]{1,0:T(8,128)(2,1)}) %all-gather.2.cloned.1.call-update) | async-done | bytes 8388624 | tf_op jit(solution)/shard_map/all_gather | solution.py:220
  393.2 14.6 %fusion.62 = f32[2048,1024]{1,0:T(8,128)} fusion(bf16[2048,2048]{1,0:T(8,128)(2,1)} %all-gather.2.cloned.1.call-done, bf16[1024,2048]{1,0:T(8,128)(2,1)} %param.26), kind=kOutput, calls=%fused_computation.123 | convolution fusion | flops 8589934592 | bytes 20971520 | tf_op jit(solution)/shard_map/dot_general | solution.py:36
  407.8 20.1 %fusion.35 = (bf16[2048,1024]{1,0:T(8,128)(2,1)S(1)}, f32[2048,1024]{1,0:T(8,128)}) fusion(f32[2048,1024]{1,0:T(8,128)} %fusion.62, bf16[2048,1024]{1,0:T(8,128)(2,1)S(1)} %copy-done.31, f32[2048,2048]{1,0:T(8,128)} %broadcast_multiply_fusion, f32[2048]{0:T(1024)S(1)} %copy-done.29), kind=kOutput, calls=%fused_computation.63 | convolution fusion | flops 8640266240 | bytes 41951232 | tf_op jit(solution)/shard_map/dot_general | solution.py:200
  429.9 11.1 convolution_convert_fusion
  443.4 124.4 %all-reduce.8.cloned.1.call-done = bf16[2048,2048]{1,0:T(8,128)(2,1)} async-done(((bf16[2048,2048]{1,0:T(8,128)(2,1)}), bf16[2048,2048]{1,0:T(8,128)(2,1)}) %all-reduce.8.cloned.1.call-update) | async-done | bytes 8388624 | tf_op jit(solution)/shard_map/psum | solution.py:225
  567.8 9.2 multiply_reduce_fusion.1
  577.0 12.6 %multiply_add_fusion = f32[2048,2048]{1,0:T(8,128)S(1)} fusion(f32[2048,2048]{1,0:T(8,128)} %broadcast_multiply_fusion, bf16[2048,2048]{1,0:T(8,128)(2,1)} %all-gather.2.cloned.1.call-done, f32[2048]{0:T(1024)S(1)} %broadcast_multiply_fusion.1, bf16[2048,2048]{1,0:T(8,128)(2,1)} %all-reduce.8.cloned.1.call-done, f32[2048]{0:T(1024)S(1)} %copy-done.29, ...), kind=kLoop, calls=%fused_computation.51 | loop fusion | flops 29360128 | bytes 50356224 | tf_op jit(solution)/shard_map/add | solution.py:229
  598.6 9.1 fusion.43
  607.8 100.7 %while.28 = (s32[]{:T(128)}, f32[2048,2,128]{0,2,1:T(8,128)S(1)}, f32[2048,2,128]{0,2,1:T(8,128)}, bf16[4,512,256]{2,1,0:T(8,128)(2,1)}, s32[4]{0:T(128)S(1)}, /...) while((s32[]{:T(128)}, f32[2048,2,128]{0,2,1:T(8,128)S(1)}, ...), condition=%wide.region_13.14_spmd.clone, body=%wide.region_11.13_spmd.clone.sunk | while | flops 2724988416 | bytes 107800928 | solution.py:134
  731.5 15.3 %convolution_convert_fusion.4 = bf16[2048,1024]{1,0:T(8,128)(2,1)} fusion(bf16[2048,1024]{1,0:T(8,128)(2,1)} %copy-done.32, f32[2048,2048]{1,0:T(8,128)} %broadcast_multiply_fusion, f32[2048]{0:T(1024)S(1)} %copy-done.30), kind=kOutput, calls=%fused_computation.74 | convolution fusion | flops 8600420352 | bytes 25174016 | tf_op jit(solution)/shard_map/dot_general | solution.py:30
  746.9 16.3 %convolution_convert_fusion.3 = bf16[1024,2048]{1,0:T(8,128)(2,1)} fusion(bf16[2048,2048]{1,0:T(8,128)(2,1)} %all-gather.2.cloned.1.call-done, f32[2048,1024]{1,0:T(8,128)} %get-tuple-element.292), kind=kOutput, calls=%fused_computation.73 | convolution fusion | flops 8610906112 | bytes 20971520 | tf_op jit(solution)/shard_map/dot_general | solution.py:30
  763.3 15.4 %convolution_convert_fusion.1 = bf16[2048,2048]{1,0:T(8,128)(2,1)} fusion(bf16[1024,2048]{1,0:T(8,128)(2,1)} %param.26, f32[2048,1024]{1,0:T(8,128)} %get-tuple-element.292), kind=kOutput, calls=%fused_computation.67 | convolution fusion | flops 8613003264 | bytes 20971520 | tf_op jit(solution)/shard_map/dot_general | solution.py:203
  780.0 8.2 fusion.64
  788.2 8.1 fusion.63
  796.3 16.5 %add_convert_fusion = bf16[2048,2048]{1,0:T(8,128)(2,1)} fusion(f32[2048,2048]{1,0:T(8,128)} %fusion.63, f32[2048,2048]{1,0:T(8,128)} %fusion.64, bf16[2048,256]{0,1:T(8,128)(2,1)S(1)} %bitcast.131, bf16[2048,256]{1,0:T(8,128)(2,1)S(1)} %copy-done.21), kind=kOutput, calls=%fused_computation.50 | convolution fusion | flops 2160066560 | bytes 44040192 | tf_op jit(solution)/shard_map/dot_general | solution.py:36
  815.2 11.3 convert_element_type.148
  826.6 11.4 convert_element_type.157
  847.6 30.6 %reduce-scatter.21.cloned.1.call-done = bf16[512,1024]{1,0:T(8,128)(2,1)} async-done(((bf16[2048,1024]{1,0:T(8,128)(2,1)}), bf16[512,1024]{1,0:T(8,128)(2,1)}) %reduce-scatter.21.cloned.1.call-update) | async-done | bytes 1048592 | tf_op jit(solution)/shard_map/reduce_scatter | solution.py:268
  881.1 76.8 %reduce-scatter.23.cloned.1.call-done = bf16[1024,512]{1,0:T(8,128)(2,1)} async-done(((bf16[1024,2048]{1,0:T(8,128)(2,1)}), bf16[1024,512]{1,0:T(8,128)(2,1)}) %reduce-scatter.23.cloned.1.call-update) | async-done | bytes 1048592 | tf_op jit(solution)/shard_map/reduce_scatter | solution.py:276
  960.7 72.3 %reduce-scatter.9.cloned.1.call-done = bf16[256,2048]{1,0:T(8,128)(2,1)} async-done(((bf16[2048,2048]{1,0:T(8,128)(2,1)}), bf16[256,2048]{1,0:T(8,128)(2,1)}) %reduce-scatter.9.cloned.1.call-update) | async-done | bytes 1048592 | tf_op jit(solution)/shard_map/reduce_scatter | solution.py:202
  1038.0 70.2 %reduce-scatter.11.cloned.1.call-done = bf16[256,2048]{1,0:T(8,128)(2,1)} async-done(((bf16[2048,2048]{1,0:T(8,128)(2,1)}), bf16[256,2048]{1,0:T(8,128)(2,1)}) %reduce-scatter.11.cloned.1.call-update) | async-done | bytes 1048592 | tf_op jit(solution)/shard_map/reduce_scatter | solution.py:245
  1110.2 39.9 %all-reduce.2 = (f32[2048]{0:T(1024)S(1)}, f32[2048]{0:T(1024)S(1)}, f32[]{:T(128)}, f32[]{:T(128)}, f32[]{:T(128)}) all-reduce(f32[2048]{0:T(1024)S(1)} %get-tuple-element.232, f32[2048]{0:T(1024)S(1)} %fusion.59, f32[]{:T(128)} %get-tuple-element.235, f32[]{:T(128)} %get-tuple-element.236, ...), channel_id=4, replica_groups=mesh['dp'=4,'mp'=8] {'dp','mp'}, use_global_device_ids=true, to_apply=%region_17.18.clone | all-reduce | flops 4099 | bytes 32792
  (298 shorter events, 259.7 us)
Async XLA Ops:
  7.2 188.9 %copy-start = (bf16[256,2048]{1,0:T(8,128)(2,1)S(1)}, bf16[256,2048]{1,0:T(8,128)(2,1)}, u32[]{:S(2)}) copy-start(bf16[256,2048]{1,0:T(8,128)(2,1)} %param.23) | copy-start | bytes 3145732
  7.2 49.8 %copy-start.8 = (bf16[256,2048]{1,0:T(8,128)(2,1)S(1)}, bf16[256,2048]{1,0:T(8,128)(2,1)}, u32[]{:S(2)}) copy-start(bf16[256,2048]{1,0:T(8,128)(2,1)} %param.16) | copy-start | bytes 3145732
  7.2 329.3 %all-reduce.6.cloned.1.call-start = ((), (), s32[]{:S(2)}) async-start(), calls=%async_computation.8 | async-start | bytes 16777216 | tf_op jit(solution)/shard_map/psum | solution.py:193
  7.3 24.7 %collective-permute-start = (bf16[256,2048]{1,0:T(8,128)(2,1)}, bf16[256,2048]{1,0:T(8,128)(2,1)S(1)}, u32[]{:S(2)}, u32[]{:S(2)}) collective-permute-start(bf16[256,2048]{1,0:T(8,128)(2,1)} %param.16), channel_id=1, source_target_pairs={{0,1},{1,2},{2,3},{3,4},{4,5},{5,6},{6,7},{7,0},{8,9},{9,10},{10,1... | collective-permute-start | bytes 3145736 | tf_op jit(solution)/shard_map/ppermute | solution.py:176
  7.8 25.8 %collective-permute-start.1 = (bf16[256,2048]{1,0:T(8,128)(2,1)}, bf16[256,2048]{1,0:T(8,128)(2,1)S(1)}, u32[]{:S(2)}, u32[]{:S(2)}) collective-permute-start(bf16[256,2048]{1,0:T(8,128)(2,1)} %param.16), channel_id=1, source_target_pairs={{0,7},{1,0},{2,1},{3,2},{4,3},{5,4},{6,5},{7,6},{8,15},{9,8},{10,9... | collective-permute-start | bytes 3145736 | tf_op jit(solution)/shard_map/ppermute | solution.py:181
  31.9 23.8 %collective-permute-start.2 = (bf16[256,2048]{1,0:T(8,128)(2,1)S(1)}, bf16[256,2048]{1,0:T(8,128)(2,1)}, u32[]{:S(2)}, u32[]{:S(2)}) collective-permute-start(bf16[256,2048]{1,0:T(8,128)(2,1)S(1)} %collective-permute-done), channel_id=1, source_target_pairs={{0,1},{1,2},{2,3},{3,4},{4,5},{5,6},{6,7},{7,0},{8,9},{9,10},{10,1... | collective-permute-start | bytes 3145736 | tf_op jit(solution)/shard_map/ppermute | solution.py:176
  33.5 24.3 %collective-permute-start.3 = (bf16[256,2048]{1,0:T(8,128)(2,1)S(1)}, bf16[256,2048]{1,0:T(8,128)(2,1)}, u32[]{:S(2)}, u32[]{:S(2)}) collective-permute-start(bf16[256,2048]{1,0:T(8,128)(2,1)S(1)} %collective-permute-done.1), channel_id=1, source_target_pairs={{0,7},{1,0},{2,1},{3,2},{4,3},{5,4},{6,5},{7,6},{8,15},{9,8},{10,9... | collective-permute-start | bytes 3145736 | tf_op jit(solution)/shard_map/ppermute | solution.py:181
  55.7 24.6 %collective-permute-start.4 = (bf16[256,2048]{1,0:T(8,128)(2,1)}, bf16[256,2048]{1,0:T(8,128)(2,1)}, u32[]{:S(2)}, u32[]{:S(2)}) collective-permute-start(bf16[256,2048]{1,0:T(8,128)(2,1)} %collective-permute-done.2), channel_id=1, source_target_pairs={{0,1},{1,2},{2,3},{3,4},{4,5},{5,6},{6,7},{7,0},{8,9},{9,10},{10,1... | collective-permute-start | bytes 3145736 | tf_op jit(solution)/shard_map/ppermute | solution.py:176
  57.8 26.6 %collective-permute-start.5 = (bf16[256,2048]{1,0:T(8,128)(2,1)}, bf16[256,2048]{1,0:T(8,128)(2,1)S(1)}, u32[]{:S(2)}, u32[]{:S(2)}) collective-permute-start(bf16[256,2048]{1,0:T(8,128)(2,1)} %collective-permute-done.3), channel_id=1, source_target_pairs={{0,7},{1,0},{2,1},{3,2},{4,3},{5,4},{6,5},{7,6},{8,15},{9,8},{10,9... | collective-permute-start | bytes 3145736 | tf_op jit(solution)/shard_map/ppermute | solution.py:181
  80.3 15.3 %collective-permute-start.6 = (bf16[256,2048]{1,0:T(8,128)(2,1)}, bf16[256,2048]{1,0:T(8,128)(2,1)S(1)}, u32[]{:S(2)}, u32[]{:S(2)}) collective-permute-start(bf16[256,2048]{1,0:T(8,128)(2,1)} %collective-permute-done.4), channel_id=1, source_target_pairs={{0,1},{1,2},{2,3},{3,4},{4,5},{5,6},{6,7},{7,0},{8,9},{9,10},{10,1... | collective-permute-start | bytes 3145736 | tf_op jit(solution)/shard_map/ppermute | solution.py:176
  81.8 19.0 %copy-start.27 = (f32[2048]{0:T(1024)S(1)}, f32[2048]{0:T(1024)}, u32[]{:S(2)}) copy-start(f32[2048]{0:T(1024)} %param.19) | copy-start | bytes 24580
  100.7 8.7 copy-start.20
  118.7 8.3 copy-start.5
  120.2 8.2 dynamic-slice-start
  203.2 190.0 %all-gather.2.cloned.1.call-start = ((), (), s32[]{:S(2)}) async-start(), calls=%async_computation.10 | async-start | bytes 9437184 | tf_op jit(solution)/shard_map/all_gather | solution.py:220
  204.0 363.8 %all-reduce.8.cloned.1.call-start = ((), (), s32[]{:S(2)}) async-start(), calls=%async_computation.11 | async-start | bytes 16777216 | tf_op jit(solution)/shard_map/psum | solution.py:225
  336.6 14.7 %copy-start.4 = (bf16[2048,2048]{1,0:T(8,128)(2,1)S(1)}, bf16[2048,2048]{1,0:T(8,128)(2,1)}, u32[]{:S(2)}) copy-start(bf16[2048,2048]{1,0:T(8,128)(2,1)} %all-reduce.6.cloned.1.call-done) | copy-start | bytes 25165828
  361.7 46.2 %copy-start.29 = (f32[2048]{0:T(1024)S(1)}, f32[2048]{0:T(1024)}, u32[]{:S(2)}) copy-start(f32[2048]{0:T(1024)} %param.24) | copy-start | bytes 24580
  393.2 14.6 %copy-start.31 = (bf16[2048,1024]{1,0:T(8,128)(2,1)S(1)}, bf16[2048,1024]{1,0:T(8,128)(2,1)}, u32[]{:S(2)}) copy-start(bf16[2048,1024]{1,0:T(8,128)(2,1)} %param.25) | copy-start | bytes 12582916
  441.0 399.4 %reduce-scatter.19.cloned.1.call-start = ((), (), s32[]{:S(2)}) async-start(), calls=%async_computation.16 | async-start | bytes 1310720 | tf_op jit(solution)/shard_map/reduce_scatter | solution.py:273
  577.0 18.3 %copy-start.12 = (bf16[4,512,256]{2,1,0:T(8,128)(2,1)S(1)}, bf16[4,512,256]{2,1,0:T(8,128)(2,1)}, u32[]{:S(2)}) copy-start(bf16[4,512,256]{2,1,0:T(8,128)(2,1)} %get-tuple-element.125) | copy-start | bytes 3145732
  607.8 234.5 %reduce-scatter.13.cloned.1.call-start = ((), (), s32[]{:S(2)}) async-start(), calls=%async_computation.13 | async-start | bytes 1310720 | tf_op jit(solution)/shard_map/reduce_scatter | solution.py:259
  715.6 128.4 %reduce-scatter.15.cloned.1.call-start = ((), (), s32[]{:S(2)}) async-start(), calls=%async_computation.14 | async-start | bytes 1310720 | tf_op jit(solution)/shard_map/reduce_scatter | solution.py:262
  722.7 123.1 %reduce-scatter.17.cloned.1.call-start = ((), (), s32[]{:S(2)}) async-start(), calls=%async_computation.15 | async-start | bytes 1310720 | tf_op jit(solution)/shard_map/reduce_scatter | solution.py:265
  731.4 146.7 %reduce-scatter.21.cloned.1.call-start = ((), (), s32[]{:S(2)}) async-start(), calls=%async_computation.17 | async-start | bytes 5242880 | tf_op jit(solution)/shard_map/reduce_scatter | solution.py:268
  746.9 211.0 %reduce-scatter.23.cloned.1.call-start = ((), (), s32[]{:S(2)}) async-start(), calls=%async_computation.18 | async-start | bytes 5242880 | tf_op jit(solution)/shard_map/reduce_scatter | solution.py:276
  763.2 269.8 %reduce-scatter.9.cloned.1.call-start = ((), (), s32[]{:S(2)}) async-start(), calls=%async_computation.9 | async-start | bytes 9437184 | tf_op jit(solution)/shard_map/reduce_scatter | solution.py:202
  778.7 329.5 %reduce-scatter.11.cloned.1.call-start = ((), (), s32[]{:S(2)}) async-start(), calls=%async_computation.12 | async-start | bytes 9437184 | tf_op jit(solution)/shard_map/reduce_scatter | solution.py:245
  780.0 8.2 copy-start.19
  780.0 8.2 copy-start.22
  840.4 267.7 %copy-start.28 = (f32[2048]{0:T(1024)S(1)}, f32[2048]{0:T(1024)}, u32[]{:S(2)}) copy-start(f32[2048]{0:T(1024)} %param.19) | copy-start | bytes 24580
  878.2 278.8 %copy-start.1 = (bf16[256,2048]{1,0:T(8,128)(2,1)S(1)}, bf16[256,2048]{1,0:T(8,128)(2,1)}, u32[]{:S(2)}) copy-start(bf16[256,2048]{1,0:T(8,128)(2,1)} %param.23) | copy-start | bytes 3145732
  (35 other events, 162.1 us)
Sparse Core Ops, SparseCore 0:
  203.4 133.1 all-reduce.5
  338.6 54.5 all-gather.1
  441.1 126.5 all-reduce.7
  607.9 27.3 reduce-scatter.18
  715.7 27.3 reduce-scatter.12
  745.8 25.7 reduce-scatter.14
  774.6 25.7 reduce-scatter.16
  802.7 75.4 reduce-scatter.20
  880.6 77.2 reduce-scatter.22
  961.2 71.7 reduce-scatter.8
  1036.9 71.2 reduce-scatter.10
